TPU v7x, 1024 devices: a whole 8x8x8 slice. The times are simulated.
1024 devices in a mesh: ctx: 64 (over y_hi, x, core), head: 16 (over y_lo, z).
Axes of the slice: x: 8, y: 8 (y_hi: 4, y_lo: 2; y = y_hi * 2 + y_lo), z: 8, core: 2. Of those that a mesh axis runs over, the one named last changes fastest.
Arguments:
- q_att: bfloat16 [16384, 2048], P('ctx', 'head'), may hold values from -6 to 6
- k_att: bfloat16 [16384, 2048], P('ctx', 'head'), may hold values from -6 to 6
- v_att: bfloat16 [16384, 2048], P('ctx', 'head'), may hold values from -6 to 6
- norm_gain: float32 [2048], P('head'), may hold values from 0.25 to 1.75
- hy_q: bfloat16 [16384, 2048], P('ctx', 'head'), may hold values from -6 to 6
- hy_k: bfloat16 [16384, 2048], P('ctx', 'head'), may hold values from -6 to 6
- feat_w: float32 [3, 7, 2048], P(None, None, 'head'), may hold values from -2 to 2
- mr_filt: float32 [128, 128], P(None, 'head'), may hold values from -0.5 to 0.5
- cotangent: bfloat16 [16384, 2048], P('ctx', 'head'), may hold values from -6 to 6
Outputs:
- output: bfloat16 [16384, 2048], P('ctx', 'head')
- grad_q: bfloat16 [16384, 2048], P('ctx', 'head')
- grad_k: bfloat16 [16384, 2048], P('ctx', 'head')
- grad_v: bfloat16 [16384, 2048], P('ctx', 'head')
All inputs are finite; a program needn't handle non-finite values.
Results may differ from a plain program's by a relative error of at most 0.019.
Values may be sent and summed in bfloat16 or wider, within the bound.
No kernel may reach another device: no remote copies, remote signals or barrier semaphores. Data moves between devices by JAX's collectives and lax.ppermute only.
A program may use at most 64 MiB of HBM per device.

v0:
```python
import functools
import math

import jax
import jax.numpy as jnp
from jax import lax
from jax.experimental import pallas as pl
from jax.experimental.pallas import tpu as pltpu
from jax.sharding import Mesh, PartitionSpec as P


HD = 128
GROUP_CH = 16
FEAT = 7
BLOCK = 256
NEGATIVE = -1e30
EPSILON = 1e-06
LOG2E = 1.4426950408889634
FACTOR = LOG2E / math.sqrt(HD)
F32 = jnp.float32
BF16 = jnp.bfloat16


VM = pl.BlockSpec(memory_space=pltpu.VMEM)
SM = pl.BlockSpec(memory_space=pltpu.SMEM)


def rounded(x):
    return x.astype(BF16).astype(F32)


def dot(a, b, dims):
    return lax.dot_general(a, b, (dims, ((), ())), preferred_element_type=F32)


def to_rows(x):
    i = lax.broadcasted_iota(jnp.int32, (128, 128), 0)
    j = lax.broadcasted_iota(jnp.int32, (128, 128), 1)
    return jnp.sum(jnp.where(i == j, x, 0.0), axis=0, keepdims=True)


def stacked(rows, height):
    at = lax.broadcasted_iota(jnp.int32, (height, 128), 0)
    out = jnp.zeros((height, 128), F32)
    for i, row in enumerate(rows):
        out = jnp.where(at == i, row, out)
    return out


def attend(info, q_ref, own_ref, oth_ref, o_ref, k_ref, v_ref, acc_ref, m_ref, s_ref, t_ref, d_ref):
    plane, column, core = info[0], info[1], info[2]

    def fill(p, c):
        for half, src in ((0, own_ref), (1, oth_ref)):
            keys = src[p, 0:256, :]
            k_ref[p, 256 * half : 256 * half + 256, :] = keys
            v_ref[p, 256 * half : 256 * half + 256, :] = jnp.concatenate(
                [src[p, 256:512, :], jnp.ones((256, 128), BF16)], axis=1
            )
        return c

    lax.fori_loop(0, plane + 1, fill, 0)

    def split(b, c):
        acc_ref[b] = jnp.zeros((256, 256), F32)
        m_ref[b] = jnp.full((256, 128), NEGATIVE, F32)
        return c

    lax.fori_loop(0, 8, split, 0)

    i = lax.broadcasted_iota(jnp.int32, (256, 256), 0)
    j = lax.broadcasted_iota(jnp.int32, (256, 256), 1)
    d_ref[...] = j - i

    def scores(n, b, p, masked):
        s = dot(q_ref[b], k_ref[p], ((1,), (1,))) * FACTOR
        if masked:
            bound = jnp.where(b > column, 512, jnp.where(b == column, 0, -512))
            seen = jnp.where(b > column, 1, jnp.where(b == column, core, 0))
            s = jnp.concatenate(
                [
                    jnp.where(d_ref[...] <= bound, s[:, 0:256], NEGATIVE),
                    jnp.where(jnp.full((256, 256), seen, jnp.int32) == 1, s[:, 256:512], NEGATIVE),
                ],
                axis=1,
            )
        s_ref[n] = s
        t_ref[n] = jnp.broadcast_to(jnp.max(s, axis=1, keepdims=True), (256, 128))

    def update(n, b, p):
        old = m_ref[b]
        new = jnp.maximum(old, rounded(t_ref[n]))
        m_ref[b] = new
        scale = jnp.exp2(old - new)
        e = jnp.concatenate([jnp.exp2(s_ref[n, :, 128 * k : 128 * k + 128] - new) for k in range(4)], axis=1)
        add = dot(e.astype(BF16), v_ref[p], ((1,), (0,)))
        acc_ref[b, :, 0:128] = acc_ref[b, :, 0:128] * scale + add[:, 0:128]
        acc_ref[b, :, 128:256] = acc_ref[b, :, 128:256] * scale + add[:, 128:256]

    def some(first, p, masked):
        for n in range(8):
            scores(n, first + n, p, masked)
            if n:
                update(n - 1, first + n - 1, p)
        update(8 - 1, first + 8 - 1, p)

    def same(g, c):
        @pl.when(8 * (g + 1) > column)
        def _():
            some(8 * g, 0, True)

        return c

    lax.fori_loop(0, 8 // 8, same, 0)

    def past(g, c):
        some(8 * lax.rem(g, 8 // 8), 1 + lax.div(g, 8 // 8), False)
        return c

    lax.fori_loop(0, plane * (8 // 8), past, 0)

    def emit(b, c):
        o_ref[b, 0:256, :] = acc_ref[b, :, 0:128].astype(BF16)
        tops, high, low = [], [], []
        for h in range(2):
            part = slice(128 * h, 128 * h + 128)
            tops.append(to_rows(m_ref[b, part, :]))
            mass = to_rows(acc_ref[b, part, 128:256])
            upper = rounded(mass)
            high.append(upper)
            low.append(mass - upper)
        o_ref[b, 256:272, :] = stacked(tops + high + low, 16).astype(BF16)
        return c

    lax.fori_loop(0, 8, emit, 0)


def combine(msg_ref, a_ref, s_ref):
    copies = s_ref.shape[0]
    n = msg_ref.shape[0]
    stats = [msg_ref[i, 256:272, :].astype(F32) for i in range(n)]
    sums = []
    for h in range(2):
        tops = [s[h : h + 1] for s in stats]
        totals = [s[2 + h : 3 + h] + s[4 + h : 5 + h] for s in stats]
        top = functools.reduce(jnp.maximum, tops)
        weights = [jnp.exp2(t - top) for t in tops]
        total = sum(w * t for w, t in zip(weights, totals))
        shares = jnp.transpose(stacked([w / total for w in weights], 128))
        out = jnp.zeros((128, 128), F32)
        for i in range(n):
            out = out + shares[:, i : i + 1] * msg_ref[i, 128 * h : 128 * h + 128, :].astype(F32)
        out = out.astype(BF16)
        a_ref[128 * h : 128 * h + 128, :] = out
        square = out.astype(F32) * out.astype(F32)
        upper = square.astype(BF16)
        lower = (square - upper.astype(F32)).astype(BF16)
        ones = jnp.ones((8, 128), BF16)
        sums.append((dot(ones, upper, ((1,), (1,))) + dot(ones, lower, ((1,), (1,))))[0:1])
    both = stacked(sums, 8)
    for i in range(copies):
        s_ref[i] = both


def normalize(a_ref, s_ref, g_ref, q_ref, k_ref, c_ref, v_ref, end_ref, begin_ref):
    n = s_ref.shape[0]
    total = functools.reduce(jnp.add, [s_ref[i] for i in range(n)])
    scale = lax.rsqrt(total * (1.0 / (n * 128)) + EPSILON)
    column = jnp.transpose(jnp.concatenate([scale, jnp.zeros((120, 128), F32)], axis=0))
    for h in range(2):
        part = slice(128 * h, 128 * h + 128)
        v_ref[part, :] = (a_ref[part, :].astype(F32) * column[:, h : h + 1] * g_ref[...]).astype(BF16)
    end_ref[0:144, :] = v_ref[112:256, :]
    end_ref[144:160, :] = q_ref[240:256, :]
    end_ref[160:304, :] = k_ref[112:256, :]
    begin_ref[0:16, :] = v_ref[0:16, :]
    begin_ref[16:160, :] = q_ref[0:144, :]
    begin_ref[160:304, :] = c_ref[0:144, :]
    begin_ref[304:320, :] = k_ref[0:16, :]


def picked(stack, rows):
    lane = lax.broadcasted_iota(jnp.int32, (rows, 128), 1) // GROUP_CH
    out = stack[0:rows]
    for g in range(1, 8):
        out = jnp.where(lane == g, stack[g * rows : (g + 1) * rows], out)
    return out


def banded(bands, data_ref):
    out = []
    for b in range(2):
        out.append(picked(dot(bands[...], data_ref[128 * b : 128 * b + 256, :], ((1,), (0,))), 128))
    tail = jnp.concatenate([bands[128 * g : 128 * g + 16, :] for g in range(8)], axis=0)
    out.append(picked(dot(tail, data_ref[256:512, :], ((1,), (0,))), 16)[0:8])
    return out


def build(f_ref, gain_ref, t_ref, bt_ref, g_ref):
    g_ref[...] = gain_ref[...]
    i = lax.broadcasted_iota(jnp.int32, (128, 128), 0)
    j = lax.broadcasted_iota(jnp.int32, (128, 128), 1)
    taps = f_ref[...].astype(BF16)
    front = dot(taps, (i + j == 128).astype(BF16), ((0,), (0,)))
    first = jnp.where(
        lax.broadcasted_iota(jnp.int32, (8, 128), 1) == 0, dot(taps, (i == 0).astype(BF16), ((0,), (0,))), 0.0
    )
    back = dot(taps, (i == j).astype(BF16), ((0,), (0,)))
    front = jnp.concatenate([front, first], axis=1)
    back = jnp.concatenate([back, jnp.zeros((8, 128), F32)], axis=1)
    for g in range(8):
        row = jnp.broadcast_to(front[g : g + 1, :], (128, 256))
        t_ref[128 * g : 128 * g + 128, :] = pltpu.roll(row, 0, 1, stride=1, stride_axis=0).astype(BF16)
        row = jnp.broadcast_to(back[g : g + 1, :], (128, 256))
        bt_ref[128 * g : 128 * g + 128, :] = pltpu.roll(row, 0, 1, stride=1, stride_axis=0).astype(BF16)


def featurized(x_ref, w_ref, index):
    total = jnp.zeros((392, 128), F32)
    for lag in range(FEAT):
        total = total + w_ref[index, lag : lag + 1, :] * x_ref[16 - lag : 408 - lag, :]
    return rounded(total)


def put(z_ref, x):
    z_ref[0:384, :] = x[0:384].astype(BF16)
    z_ref[384:400, :] = jnp.concatenate([x[384:392], jnp.zeros((8, 128), F32)], axis=0).astype(BF16)
    z_ref[400:512, :] = jnp.zeros((112, 128), BF16)


def finish(
    v_ref, q_ref, k_ref, c_ref, before_ref, after_ref, w_ref, t_ref, bt_ref,
    o_ref, gq_ref, gk_ref, gv_ref,
    x_ref, y_ref, s_ref, e_ref, m_ref, n_ref, a_ref, b_ref, d_ref, h_ref,
):
    y_ref[0:16, :] = before_ref[144:160, :].astype(F32)
    y_ref[16:272, :] = q_ref[...].astype(F32)
    y_ref[272:416, :] = after_ref[16:160, :].astype(F32)
    qf = featurized(y_ref, w_ref, 0)
    e_ref[0:256, :] = c_ref[...].astype(F32)
    e_ref[256:400, :] = after_ref[160:304, :].astype(F32)
    put(n_ref, e_ref[0:392, :] * qf)
    x_ref[0:144, :] = before_ref[160:304, :].astype(F32)
    x_ref[144:400, :] = k_ref[...].astype(F32)
    x_ref[400:416, :] = after_ref[304:320, :].astype(F32)
    kf = featurized(x_ref, w_ref, 1)
    s_ref[0:144, :] = before_ref[0:144, :].astype(F32)
    s_ref[144:400, :] = v_ref[...].astype(F32)
    s_ref[400:416, :] = after_ref[0:16, :].astype(F32)
    vf = featurized(s_ref, w_ref, 2)
    put(m_ref, kf * vf)
    for b, back in enumerate(banded(bt_ref, n_ref)):
        d_ref[128 * b : 128 * b + back.shape[0], :] = back
    for b, signal in enumerate(banded(t_ref, m_ref)):
        part = slice(128 * b, 128 * b + signal.shape[0])
        if b < 2:
            o_ref[part, :] = (qf[part] * signal).astype(BF16)
        a_ref[part, :] = rounded(e_ref[part, :] * signal)
    b_ref[...] = rounded(d_ref[...] * vf[128:392])
    h_ref[...] = rounded(d_ref[...] * kf[128:392])
    for i, (src, dst) in enumerate(((a_ref, gq_ref), (b_ref, gk_ref), (h_ref, gv_ref))):
        total = jnp.zeros((256, 128), F32)
        for lag in range(FEAT):
            total = total + w_ref[i, lag : lag + 1, :] * src[lag : lag + 256, :]
        dst[...] = total.astype(BF16)


def shape(dims, dtype=BF16):
    return jax.ShapeDtypeStruct(dims, dtype)


def call(body, outs, args, scratch=(), specs=None, flops=0, size=1 << 20, limit=8):
    single = not isinstance(outs, (list, tuple))
    return pl.pallas_call(
        body,
        out_shape=outs,
        in_specs=specs or [VM] * len(args),
        out_specs=VM if single else [VM] * len(outs),
        scratch_shapes=list(scratch),
        cost_estimate=pl.CostEstimate(flops=flops, bytes_accessed=size, transcendentals=0),
        compiler_params=pltpu.CompilerParams(vmem_limit_bytes=limit << 20),
    )(*args)


CTX = ("y_hi", "x", "core")
HEAD = ("y_lo", "z")


def neighbour(block, distance):
    n = lax.axis_size(CTX)
    return lax.ppermute(block, CTX, [(i, i + distance) for i in range(n) if 0 <= i + distance < n])


def per_device(q_att, k_att, v_att, norm_gain, hy_q, hy_k, feat_w, mr_filt, cotangent):
    info = jnp.stack([lax.axis_index("y_hi"), lax.axis_index("x"), lax.axis_index("core"), 0]).astype(jnp.int32)
    both = jnp.concatenate([k_att, v_att], axis=0)
    came = []
    for d in (1, 2, 3):
        came.append(lax.ppermute(both, "y_hi", [(i, i + d) for i in range(4 - d)]))
    rows = lax.all_to_all(jnp.broadcast_to(q_att[None], (8, BLOCK, HD)), "x", 0, 0, tiled=True)
    own = jnp.stack([both] + came)
    other = lax.ppermute(own, "core", [(0, 1), (1, 0)])
    bands, back_bands, gain = call(
        build, [shape((1024, 256))] * 2 + [shape((1, 128), F32)], (mr_filt, norm_gain[None]), flops=4 * 10**8
    )
    info, rows, own, other, bands, back_bands, gain = lax.optimization_barrier(
        (info, rows, own, other, bands, back_bands, gain)
    )
    partial = call(
        attend,
        shape((8, 272, 128)),
        (info, rows, own, other),
        [
            pltpu.VMEM((4, 512, 128), BF16),
            pltpu.VMEM((4, 512, 256), BF16),
            pltpu.VMEM((8, 256, 256), F32),
            pltpu.VMEM((8, 256, 128), F32),
            pltpu.VMEM((8, 256, 512), F32),
            pltpu.VMEM((8, 256, 128), F32),
            pltpu.VMEM((256, 256), jnp.int32),
        ],
        specs=[SM, VM, VM, VM],
        flops=4 * 10**9,
        limit=24,
    )
    parts = lax.all_to_all(partial, "x", 0, 0, tiled=True)
    attended, sums = call(combine, [shape((256, 128)), shape((16, 8, 128), F32)], (parts,))
    squares = lax.all_to_all(sums, HEAD, 0, 0, tiled=True)
    value, end, begin = call(
        normalize,
        [shape((256, 128)), shape((304, 128)), shape((320, 128))],
        (attended, squares, gain, hy_q, hy_k, cotangent),
    )
    before = neighbour(end, 1)
    after = neighbour(begin, -1)
    tall = pltpu.VMEM((416, 128), F32)
    return tuple(
        call(
            finish,
            [shape((256, 128))] * 4,
            (value, hy_q, hy_k, cotangent, before, after, feat_w, bands, back_bands),
            [tall] * 4 + [pltpu.VMEM((512, 128), BF16)] * 2 + [pltpu.VMEM((264, 128), F32)] * 4,
        )
    )


def solution(mesh):
    fine = Mesh(mesh.devices.reshape(4, 8, 2, 2, 8), CTX + HEAD)
    tokens = P(CTX, HEAD)
    placed = (tokens, tokens, tokens, P(HEAD), tokens, tokens, P(None, None, HEAD), P(None, HEAD), tokens)
    return jax.shard_map(per_device, mesh=fine, in_specs=placed, out_specs=(tokens,) * 4, check_vma=False)
```

profile of v0, /device:TPU:64, one launch (start us, length us, event | category | flops | bytes accessed | tf_op | source)
XLA Modules:
  0.0 106.1 jit_solution(274785607984317531)
XLA Ops:
  0.6 1.7 %broadcast_in_dim.4 = bf16[8,256,128]{2,1,0:T(8,128)(2,1)} broadcast(bf16[256,128]{1,0:T(8,128)(2,1)} %param.9), dimensions={1,2} | broadcast | bytes 589824 | tf_op jit(solution)/shard_map/broadcast_in_dim | solution.py:300
  2.3 6.9 %all-to-all-start = ((bf16[8,256,128]{2,1,0:T(8,128)(2,1)}), bf16[8,256,128]{2,1,0:T(8,128)(2,1)S(1)}, u32[]{:S(2)}, u32[]{:S(2)}) async-start(bf16[8,256,128]{2,1,0:T(8,128)(2,1)} %broadcast_in_dim.4), calls=%async_computation | async-start | bytes 1048576 | tf_op jit(solution)/shard_map/all_to_all | solution.py:300
  9.2 0.0 copy-start.6
  9.3 0.8 copy-done.6
  10.1 0.7 collective-permute-start.2
  10.8 1.3 %collective-permute-start.1 = (bf16[512,128]{1,0:T(8,128)(2,1)S(1)}, bf16[512,128]{1,0:T(8,128)(2,1)S(1)}, u32[]{:S(2)}, u32[]{:S(2)}) collective-permute-start(bf16[512,128]{1,0:T(8,128)(2,1)S(1)} %constant_dynamic-update-slice_fusion), channel_id=1, source_target_pairs={{0,512},{256,768},{1,513},{257,769},{2,514},{258,770},{3,515},{259... | collective-permute-start | bytes 393224 | tf_op jit(solution)/shard_map/ppermute | solution.py:299
  12.1 3.5 %collective-permute-start = (bf16[512,128]{1,0:T(8,128)(2,1)S(1)}, bf16[512,128]{1,0:T(8,128)(2,1)S(1)}, u32[]{:S(2)}, u32[]{:S(2)}) collective-permute-start(bf16[512,128]{1,0:T(8,128)(2,1)S(1)} %constant_dynamic-update-slice_fusion), channel_id=1, source_target_pairs={{0,256},{256,512},{512,768},{1,257},{257,513},{513,769},{2,258},{2... | collective-permute-start | bytes 393224 | tf_op jit(solution)/shard_map/ppermute | solution.py:299
  15.6 0.0 collective-permute-done.2
  15.6 10.4 %collective-permute-done.1 = bf16[512,128]{1,0:T(8,128)(2,1)S(1)} collective-permute-done((bf16[512,128]{1,0:T(8,128)(2,1)S(1)}, bf16[512,128]{1,0:T(8,128)(2,1)S(1)}, u32[]{:S(2)}, u32[]{:S(2)}) %collective-permute-start.1) | collective-permute-done | bytes 131104 | tf_op jit(solution)/shard_map/ppermute | solution.py:299
  26.1 3.2 %collective-permute-done = bf16[512,128]{1,0:T(8,128)(2,1)S(1)} collective-permute-done((bf16[512,128]{1,0:T(8,128)(2,1)S(1)}, bf16[512,128]{1,0:T(8,128)(2,1)S(1)}, u32[]{:S(2)}, u32[]{:S(2)}) %collective-permute-start) | collective-permute-done | bytes 131104 | tf_op jit(solution)/shard_map/ppermute | solution.py:299
  29.3 0.1 pad_maximum_fusion.own_ref
  29.4 1.9 %collective-permute-start.3 = (bf16[4,512,128]{2,1,0:T(8,128)(2,1)S(1)}, bf16[4,512,128]{2,1,0:T(8,128)(2,1)S(1)}, u32[]{:S(2)}, u32[]{:S(2)}) collective-permute-start(bf16[4,512,128]{2,1,0:T(8,128)(2,1)S(1)} %pad_maximum_fusion.own_ref), channel_id=1, source_target_pairs={{0,16},{16,0},{1,17},{17,1},{2,18},{18,2},{3,19},{19,3},{4,20},{20... | collective-permute-start | bytes 1572872 | tf_op jit(solution)/shard_map/ppermute | solution.py:302
  31.3 0.0 copy-start.7
  31.3 0.7 copy-done.7
  32.0 0.1 copy.13.f_ref
  32.1 0.7 copy-done.4
  32.7 0.5 shard_map.120
  33.3 0.1 pad_add_fusion.info
  33.3 0.0 collective-permute-done.3.oth_ref
  33.3 0.0 all-to-all-done.q_ref
  33.3 5.7 %shard_map.121 = bf16[8,272,128]{2,1,0:T(8,128)(2,1)S(1)} custom-call(s32[4]{0:T(128)S(1)} %pad_add_fusion.info, bf16[8,256,128]{2,1,0:T(8,128)(2,1)S(1)} %all-to-all-done.q_ref, bf16[4,512,128]{2,1,0:T(8,128)(2,1)S(1)} %pad_maximum_fusion.own_ref, bf16[4,512,128]{2,1,0:T(8,128)(2,1)S(1)} %collective-permute-done.3.oth_ref), custom_call_target="tpu_custom_call" | custom-call | flops 4000000000 | bytes 1048576 | tf_op jit(solution)/shard_map/pallas_call | solution.py:274
  39.1 25.6 %all_to_all.15.msg_ref = bf16[8,272,128]{2,1,0:T(8,128)(2,1)S(1)} all-to-all(bf16[8,272,128]{2,1,0:T(8,128)(2,1)S(1)} %shard_map.121), channel_id=1, replica_groups=mesh['y_hi'=4,'x'=8,'core'=2,'y_lo'=2,'z'=8] {'x'}, dimensions={0} | all-to-all | bytes 1114112 | tf_op jit(solution)/shard_map/all_to_all | solution.py:326
  64.7 0.7 shard_map.122
  65.3 0.0 copy-start.1
  65.4 26.8 %all_to_all.16.s_ref = f32[16,8,128]{2,1,0:T(8,128)S(1)} all-to-all(f32[16,8,128]{2,1,0:T(8,128)S(1)} %get-tuple-element.27), channel_id=1, replica_groups=mesh['y_hi'=4,'x'=8,'core'=2,'y_lo'=2,'z'=8] {'y_lo','z'}, dimensions={0} | all-to-all | bytes 131072 | tf_op jit(solution)/shard_map/all_to_all | solution.py:328
  92.2 0.0 copy-start.3
  92.3 0.2 shard_map.123
  92.5 1.9 %collective-permute-start.5 = (bf16[320,128]{1,0:T(8,128)(2,1)S(1)}, bf16[320,128]{1,0:T(8,128)(2,1)S(1)}, u32[]{:S(2)}, u32[]{:S(2)}) collective-permute-start(bf16[320,128]{1,0:T(8,128)(2,1)S(1)} %get-tuple-element.31), channel_id=1, source_target_pairs={{16,0},{32,16},{48,32},{64,48},{80,64},{96,80},{112,96},{128,112},... | collective-permute-start | bytes 245768 | tf_op jit(solution)/shard_map/ppermute | solution.py:291
  94.4 2.4 %collective-permute-start.4 = (bf16[304,128]{1,0:T(8,128)(2,1)S(1)}, bf16[304,128]{1,0:T(8,128)(2,1)S(1)}, u32[]{:S(2)}, u32[]{:S(2)}) collective-permute-start(bf16[304,128]{1,0:T(8,128)(2,1)S(1)} %get-tuple-element.30), channel_id=1, source_target_pairs={{0,16},{16,32},{32,48},{48,64},{64,80},{80,96},{96,112},{112,128},... | collective-permute-start | bytes 233480 | tf_op jit(solution)/shard_map/ppermute | solution.py:291
  96.8 7.5 %collective-permute-done.4.before_ref = bf16[304,128]{1,0:T(8,128)(2,1)S(1)} collective-permute-done((bf16[304,128]{1,0:T(8,128)(2,1)S(1)}, bf16[304,128]{1,0:T(8,128)(2,1)S(1)}, u32[]{:S(2)}, u32[]{:S(2)}) %collective-permute-start.4) | collective-permute-done | bytes 77856 | tf_op jit(solution)/shard_map/ppermute | solution.py:291
  104.4 0.0 collective-permute-done.5.after_ref
  104.4 1.7 %shard_map.124 = (bf16[256,128]{1,0:T(8,128)(2,1)}, bf16[256,128]{1,0:T(8,128)(2,1)}, bf16[256,128]{1,0:T(8,128)(2,1)}, bf16[256,128]{1,0:T(8,128)(2,1)}) custom-call(bf16[256,128]{1,0:T(8,128)(2,1)S(1)} %get-tuple-element.29.v_ref, bf16[256,128]{1,0:T(8,128)(2,1)S(1)} %copy-done, bf16[256,128]{1,0:T(8,128)(2,1)S(1)} %copy-done.1, ...), custom_call_target="tpu_custom_call" | custom-call | bytes 1048576 | tf_op jit(solution)/shard_map/pallas_call | solution.py:274
  (11 shorter events, 0.0 us)
Async XLA Ops:
  2.3 6.9 %copy-start.5 = (bf16[256,128]{1,0:T(8,128)(2,1)S(1)}, bf16[256,128]{1,0:T(8,128)(2,1)}, u32[]{:S(2)}) copy-start(bf16[256,128]{1,0:T(8,128)(2,1)} %param.10) | copy-start | bytes 196612
  2.3 31.0 %all-to-all-start = ((bf16[8,256,128]{2,1,0:T(8,128)(2,1)}), bf16[8,256,128]{2,1,0:T(8,128)(2,1)S(1)}, u32[]{:S(2)}, u32[]{:S(2)}) async-start(bf16[8,256,128]{2,1,0:T(8,128)(2,1)} %broadcast_in_dim.4), calls=%async_computation | async-start | bytes 1048576 | tf_op jit(solution)/shard_map/all_to_all | solution.py:300
  9.2 0.8 copy-start.6
  10.1 5.5 %collective-permute-start.2 = (bf16[512,128]{1,0:T(8,128)(2,1)S(1)}, bf16[512,128]{1,0:T(8,128)(2,1)S(1)}, u32[]{:S(2)}, u32[]{:S(2)}) collective-permute-start(bf16[512,128]{1,0:T(8,128)(2,1)S(1)} %constant_dynamic-update-slice_fusion), channel_id=1, source_target_pairs={{0,768},{1,769},{2,770},{3,771},{4,772},{5,773},{6,774},{7,775},{8... | collective-permute-start | bytes 393224 | tf_op jit(solution)/shard_map/ppermute | solution.py:299
  10.8 15.3 %collective-permute-start.1 = (bf16[512,128]{1,0:T(8,128)(2,1)S(1)}, bf16[512,128]{1,0:T(8,128)(2,1)S(1)}, u32[]{:S(2)}, u32[]{:S(2)}) collective-permute-start(bf16[512,128]{1,0:T(8,128)(2,1)S(1)} %constant_dynamic-update-slice_fusion), channel_id=1, source_target_pairs={{0,512},{256,768},{1,513},{257,769},{2,514},{258,770},{3,515},{259... | collective-permute-start | bytes 393224 | tf_op jit(solution)/shard_map/ppermute | solution.py:299
  12.1 17.2 %collective-permute-start = (bf16[512,128]{1,0:T(8,128)(2,1)S(1)}, bf16[512,128]{1,0:T(8,128)(2,1)S(1)}, u32[]{:S(2)}, u32[]{:S(2)}) collective-permute-start(bf16[512,128]{1,0:T(8,128)(2,1)S(1)} %constant_dynamic-update-slice_fusion), channel_id=1, source_target_pairs={{0,256},{256,512},{512,768},{1,257},{257,513},{513,769},{2,258},{2... | collective-permute-start | bytes 393224 | tf_op jit(solution)/shard_map/ppermute | solution.py:299
  29.4 4.0 %collective-permute-start.3 = (bf16[4,512,128]{2,1,0:T(8,128)(2,1)S(1)}, bf16[4,512,128]{2,1,0:T(8,128)(2,1)S(1)}, u32[]{:S(2)}, u32[]{:S(2)}) collective-permute-start(bf16[4,512,128]{2,1,0:T(8,128)(2,1)S(1)} %pad_maximum_fusion.own_ref), channel_id=1, source_target_pairs={{0,16},{16,0},{1,17},{17,1},{2,18},{18,2},{3,19},{19,3},{4,20},{20... | collective-permute-start | bytes 1572872 | tf_op jit(solution)/shard_map/ppermute | solution.py:302
  31.3 0.7 copy-start.7
  32.1 0.7 copy-start.4
  64.7 27.6 %copy-start.2 = (bf16[256,128]{1,0:T(8,128)(2,1)S(1)}, bf16[256,128]{1,0:T(8,128)(2,1)}, u32[]{:S(2)}) copy-start(bf16[256,128]{1,0:T(8,128)(2,1)} %c_ref.3) | copy-start | bytes 196612
  65.3 26.9 %copy-start = (bf16[256,128]{1,0:T(8,128)(2,1)S(1)}, bf16[256,128]{1,0:T(8,128)(2,1)}, u32[]{:S(2)}) copy-start(bf16[256,128]{1,0:T(8,128)(2,1)} %q_ref.3) | copy-start | bytes 196612
  65.3 26.9 %copy-start.1 = (bf16[256,128]{1,0:T(8,128)(2,1)S(1)}, bf16[256,128]{1,0:T(8,128)(2,1)}, u32[]{:S(2)}) copy-start(bf16[256,128]{1,0:T(8,128)(2,1)} %k_ref.3) | copy-start | bytes 196612
  92.2 12.1 %copy-start.3 = (f32[3,7,128]{2,1,0:T(8,128)S(1)}, f32[3,7,128]{2,1,0:T(8,128)}, u32[]{:S(2)}) copy-start(f32[3,7,128]{2,1,0:T(8,128)} %w_ref.1) | copy-start | bytes 32260
  92.5 11.9 %collective-permute-start.5 = (bf16[320,128]{1,0:T(8,128)(2,1)S(1)}, bf16[320,128]{1,0:T(8,128)(2,1)S(1)}, u32[]{:S(2)}, u32[]{:S(2)}) collective-permute-start(bf16[320,128]{1,0:T(8,128)(2,1)S(1)} %get-tuple-element.31), channel_id=1, source_target_pairs={{16,0},{32,16},{48,32},{64,48},{80,64},{96,80},{112,96},{128,112},... | collective-permute-start | bytes 245768 | tf_op jit(solution)/shard_map/ppermute | solution.py:291
  94.4 9.9 %collective-permute-start.4 = (bf16[304,128]{1,0:T(8,128)(2,1)S(1)}, bf16[304,128]{1,0:T(8,128)(2,1)S(1)}, u32[]{:S(2)}, u32[]{:S(2)}) collective-permute-start(bf16[304,128]{1,0:T(8,128)(2,1)S(1)} %get-tuple-element.30), channel_id=1, source_target_pairs={{0,16},{16,32},{32,48},{48,64},{64,80},{80,96},{96,112},{112,128},... | collective-permute-start | bytes 233480 | tf_op jit(solution)/shard_map/ppermute | solution.py:291
where the time goes:
time: 107 us; the launch traced here: 106 us
  blocking collectives  52.4 us (49%)
  waiting for transfers between devices  21.2 us (20%)
  starting transfers between devices  18.6 us (17%)
  Pallas kernels  8.93 us (8%)
  local copies, waits for them, and re-layouts  4.03 us (4%)
    all_to_all x1, blocking collectives, per_device(): squares = lax.all_to_all(sums, HEAD, 0, 0, tiled=True)  26.8 us
    all_to_all x1, blocking collectives, per_device(): parts = lax.all_to_all(partial, 'x', 0, 0, tiled=True)  25.6 us
    ppermute x3, waiting for transfers between devices, per_device(): came.append(lax.ppermute(both, 'y_hi', [(i, i + d) for i in range(4 - d)]))  13.6 us
    pallas_call x5, Pallas kernels, call(): pl.pallas_call(body, out_shape=outs, in_specs=specs or [VM] * len(args),...  8.93 us
    ppermute x2, waiting for transfers between devices, neighbour(): lax.ppermute(block, CTX, [(i, i + distance) for i in range(n) if 0 <= i +...  7.52 us
    all_to_all x1, starting transfers between devices, per_device(): lax.all_to_all(jnp.broadcast_to(q_att[None], (8, BLOCK, HD)), 'x', 0, 0,...  6.89 us
    ppermute x3, starting transfers between devices, per_device(): came.append(lax.ppermute(both, 'y_hi', [(i, i + d) for i in range(4 - d)]))  5.51 us
    ppermute x2, starting transfers between devices, neighbour(): lax.ppermute(block, CTX, [(i, i + distance) for i in range(n) if 0 <= i +...  4.33 us
  transfers between devices with their start and end apart: 7, of which 3 were waited for; matrix products, arithmetic and copies ran while one was open for 0% of the time, Pallas kernels for 0%

commit v1 on v0

--- a/solution.py
+++ b/solution.py
@@ -129,7 +129,7 @@
             upper = rounded(mass)
             high.append(upper)
             low.append(mass - upper)
-        o_ref[b, 256:272, :] = stacked(tops + high + low, 16).astype(BF16)
+        o_ref[b, 256:264, :] = stacked(tops + high + low, 8).astype(BF16)
         return c
 
     lax.fori_loop(0, 8, emit, 0)
@@ -138,7 +138,7 @@
 def combine(msg_ref, a_ref, s_ref):
     copies = s_ref.shape[0]
     n = msg_ref.shape[0]
-    stats = [msg_ref[i, 256:272, :].astype(F32) for i in range(n)]
+    stats = [msg_ref[i, 256:264, :].astype(F32) for i in range(n)]
     sums = []
     for h in range(2):
         tops = [s[h : h + 1] for s in stats]
@@ -308,7 +308,7 @@
     )
     partial = call(
         attend,
-        shape((8, 272, 128)),
+        shape((8, 264, 128)),
         (info, rows, own, other),
         [
             pltpu.VMEM((4, 512, 128), BF16),

time: 107 us -> 106 us (level)
  no operation moved by 1% of the time
where the time goes in v1:
time: 106 us
  blocking collectives  52.1 us (49%)
  waiting for transfers between devices  21.2 us (20%)
  starting transfers between devices  18.6 us (18%)
  Pallas kernels  8.91 us (8%)
  local copies, waits for them, and re-layouts  4.03 us (4%)
    all_to_all x1, blocking collectives, per_device(): squares = lax.all_to_all(sums, HEAD, 0, 0, tiled=True)  26.8 us
    all_to_all x1, blocking collectives, per_device(): parts = lax.all_to_all(partial, 'x', 0, 0, tiled=True)  25.2 us
    ppermute x3, waiting for transfers between devices, per_device(): came.append(lax.ppermute(both, 'y_hi', [(i, i + d) for i in range(4 - d)]))  13.6 us
    pallas_call x5, Pallas kernels, call(): pl.pallas_call(body, out_shape=outs, in_specs=specs or [VM] * len(args),...  8.91 us
    ppermute x2, waiting for transfers between devices, neighbour(): lax.ppermute(block, CTX, [(i, i + distance) for i in range(n) if 0 <= i +...  7.52 us
    all_to_all x1, starting transfers between devices, per_device(): lax.all_to_all(jnp.broadcast_to(q_att[None], (8, BLOCK, HD)), 'x', 0, 0,...  6.89 us
    ppermute x3, starting transfers between devices, per_device(): came.append(lax.ppermute(both, 'y_hi', [(i, i + d) for i in range(4 - d)]))  5.51 us
    ppermute x2, starting transfers between devices, neighbour(): lax.ppermute(block, CTX, [(i, i + distance) for i in range(n) if 0 <= i +...  4.33 us
  transfers between devices with their start and end apart: 7, of which 3 were waited for; matrix products, arithmetic and copies ran while one was open for 0% of the time, Pallas kernels for 0%

profile of v1, /device:TPU:64, one launch (start us, length us, event | category | flops | bytes accessed | tf_op | source)
XLA Modules:
  0.0 105.7 jit_solution(11531148426625711377)
XLA Ops:
  0.6 1.7 %broadcast_in_dim.4 = bf16[8,256,128]{2,1,0:T(8,128)(2,1)} broadcast(bf16[256,128]{1,0:T(8,128)(2,1)} %param.9), dimensions={1,2} | broadcast | bytes 589824 | tf_op jit(solution)/shard_map/broadcast_in_dim | solution.py:300
  2.3 6.9 %all-to-all-start = ((bf16[8,256,128]{2,1,0:T(8,128)(2,1)}), bf16[8,256,128]{2,1,0:T(8,128)(2,1)S(1)}, u32[]{:S(2)}, u32[]{:S(2)}) async-start(bf16[8,256,128]{2,1,0:T(8,128)(2,1)} %broadcast_in_dim.4), calls=%async_computation | async-start | bytes 1048576 | tf_op jit(solution)/shard_map/all_to_all | solution.py:300
  9.2 0.0 copy-start.6
  9.3 0.8 copy-done.6
  10.1 0.7 collective-permute-start.2
  10.8 1.3 %collective-permute-start.1 = (bf16[512,128]{1,0:T(8,128)(2,1)S(1)}, bf16[512,128]{1,0:T(8,128)(2,1)S(1)}, u32[]{:S(2)}, u32[]{:S(2)}) collective-permute-start(bf16[512,128]{1,0:T(8,128)(2,1)S(1)} %constant_dynamic-update-slice_fusion), channel_id=1, source_target_pairs={{0,512},{256,768},{1,513},{257,769},{2,514},{258,770},{3,515},{259... | collective-permute-start | bytes 393224 | tf_op jit(solution)/shard_map/ppermute | solution.py:299
  12.1 3.5 %collective-permute-start = (bf16[512,128]{1,0:T(8,128)(2,1)S(1)}, bf16[512,128]{1,0:T(8,128)(2,1)S(1)}, u32[]{:S(2)}, u32[]{:S(2)}) collective-permute-start(bf16[512,128]{1,0:T(8,128)(2,1)S(1)} %constant_dynamic-update-slice_fusion), channel_id=1, source_target_pairs={{0,256},{256,512},{512,768},{1,257},{257,513},{513,769},{2,258},{2... | collective-permute-start | bytes 393224 | tf_op jit(solution)/shard_map/ppermute | solution.py:299
  15.6 0.0 collective-permute-done.2
  15.6 10.4 %collective-permute-done.1 = bf16[512,128]{1,0:T(8,128)(2,1)S(1)} collective-permute-done((bf16[512,128]{1,0:T(8,128)(2,1)S(1)}, bf16[512,128]{1,0:T(8,128)(2,1)S(1)}, u32[]{:S(2)}, u32[]{:S(2)}) %collective-permute-start.1) | collective-permute-done | bytes 131104 | tf_op jit(solution)/shard_map/ppermute | solution.py:299
  26.1 3.2 %collective-permute-done = bf16[512,128]{1,0:T(8,128)(2,1)S(1)} collective-permute-done((bf16[512,128]{1,0:T(8,128)(2,1)S(1)}, bf16[512,128]{1,0:T(8,128)(2,1)S(1)}, u32[]{:S(2)}, u32[]{:S(2)}) %collective-permute-start) | collective-permute-done | bytes 131104 | tf_op jit(solution)/shard_map/ppermute | solution.py:299
  29.3 0.1 pad_maximum_fusion.own_ref
  29.4 1.9 %collective-permute-start.3 = (bf16[4,512,128]{2,1,0:T(8,128)(2,1)S(1)}, bf16[4,512,128]{2,1,0:T(8,128)(2,1)S(1)}, u32[]{:S(2)}, u32[]{:S(2)}) collective-permute-start(bf16[4,512,128]{2,1,0:T(8,128)(2,1)S(1)} %pad_maximum_fusion.own_ref), channel_id=1, source_target_pairs={{0,16},{16,0},{1,17},{17,1},{2,18},{18,2},{3,19},{19,3},{4,20},{20... | collective-permute-start | bytes 1572872 | tf_op jit(solution)/shard_map/ppermute | solution.py:302
  31.3 0.0 copy-start.7
  31.3 0.7 copy-done.7
  32.0 0.1 copy.13.f_ref
  32.1 0.7 copy-done.4
  32.7 0.5 shard_map.120
  33.3 0.1 pad_add_fusion.info
  33.3 0.0 collective-permute-done.3.oth_ref
  33.3 0.0 all-to-all-done.q_ref
  33.3 5.7 %shard_map.121 = bf16[8,264,128]{2,1,0:T(8,128)(2,1)S(1)} custom-call(s32[4]{0:T(128)S(1)} %pad_add_fusion.info, bf16[8,256,128]{2,1,0:T(8,128)(2,1)S(1)} %all-to-all-done.q_ref, bf16[4,512,128]{2,1,0:T(8,128)(2,1)S(1)} %pad_maximum_fusion.own_ref, bf16[4,512,128]{2,1,0:T(8,128)(2,1)S(1)} %collective-permute-done.3.oth_ref), custom_call_target="tpu_custom_call" | custom-call | flops 4000000000 | bytes 1048576 | tf_op jit(solution)/shard_map/pallas_call | solution.py:274
  39.1 25.2 %all_to_all.15.msg_ref = bf16[8,264,128]{2,1,0:T(8,128)(2,1)S(1)} all-to-all(bf16[8,264,128]{2,1,0:T(8,128)(2,1)S(1)} %shard_map.121), channel_id=1, replica_groups=mesh['y_hi'=4,'x'=8,'core'=2,'y_lo'=2,'z'=8] {'x'}, dimensions={0} | all-to-all | bytes 1081344 | tf_op jit(solution)/shard_map/all_to_all | solution.py:326
  64.3 0.7 shard_map.122
  65.0 0.0 copy-start.1
  65.0 26.8 %all_to_all.16.s_ref = f32[16,8,128]{2,1,0:T(8,128)S(1)} all-to-all(f32[16,8,128]{2,1,0:T(8,128)S(1)} %get-tuple-element.27), channel_id=1, replica_groups=mesh['y_hi'=4,'x'=8,'core'=2,'y_lo'=2,'z'=8] {'y_lo','z'}, dimensions={0} | all-to-all | bytes 131072 | tf_op jit(solution)/shard_map/all_to_all | solution.py:328
  91.9 0.0 copy-start.3
  91.9 0.2 shard_map.123
  92.2 1.9 %collective-permute-start.5 = (bf16[320,128]{1,0:T(8,128)(2,1)S(1)}, bf16[320,128]{1,0:T(8,128)(2,1)S(1)}, u32[]{:S(2)}, u32[]{:S(2)}) collective-permute-start(bf16[320,128]{1,0:T(8,128)(2,1)S(1)} %get-tuple-element.31), channel_id=1, source_target_pairs={{16,0},{32,16},{48,32},{64,48},{80,64},{96,80},{112,96},{128,112},... | collective-permute-start | bytes 245768 | tf_op jit(solution)/shard_map/ppermute | solution.py:291
  94.1 2.4 %collective-permute-start.4 = (bf16[304,128]{1,0:T(8,128)(2,1)S(1)}, bf16[304,128]{1,0:T(8,128)(2,1)S(1)}, u32[]{:S(2)}, u32[]{:S(2)}) collective-permute-start(bf16[304,128]{1,0:T(8,128)(2,1)S(1)} %get-tuple-element.30), channel_id=1, source_target_pairs={{0,16},{16,32},{32,48},{48,64},{64,80},{80,96},{96,112},{112,128},... | collective-permute-start | bytes 233480 | tf_op jit(solution)/shard_map/ppermute | solution.py:291
  96.5 7.5 %collective-permute-done.4.before_ref = bf16[304,128]{1,0:T(8,128)(2,1)S(1)} collective-permute-done((bf16[304,128]{1,0:T(8,128)(2,1)S(1)}, bf16[304,128]{1,0:T(8,128)(2,1)S(1)}, u32[]{:S(2)}, u32[]{:S(2)}) %collective-permute-start.4) | collective-permute-done | bytes 77856 | tf_op jit(solution)/shard_map/ppermute | solution.py:291
  104.0 0.0 collective-permute-done.5.after_ref
  104.0 1.7 %shard_map.124 = (bf16[256,128]{1,0:T(8,128)(2,1)}, bf16[256,128]{1,0:T(8,128)(2,1)}, bf16[256,128]{1,0:T(8,128)(2,1)}, bf16[256,128]{1,0:T(8,128)(2,1)}) custom-call(bf16[256,128]{1,0:T(8,128)(2,1)S(1)} %get-tuple-element.29.v_ref, bf16[256,128]{1,0:T(8,128)(2,1)S(1)} %copy-done, bf16[256,128]{1,0:T(8,128)(2,1)S(1)} %copy-done.1, ...), custom_call_target="tpu_custom_call" | custom-call | bytes 1048576 | tf_op jit(solution)/shard_map/pallas_call | solution.py:274
  (11 shorter events, 0.0 us)
Async XLA Ops:
  2.3 6.9 %copy-start.5 = (bf16[256,128]{1,0:T(8,128)(2,1)S(1)}, bf16[256,128]{1,0:T(8,128)(2,1)}, u32[]{:S(2)}) copy-start(bf16[256,128]{1,0:T(8,128)(2,1)} %param.10) | copy-start | bytes 196612
  2.3 31.0 %all-to-all-start = ((bf16[8,256,128]{2,1,0:T(8,128)(2,1)}), bf16[8,256,128]{2,1,0:T(8,128)(2,1)S(1)}, u32[]{:S(2)}, u32[]{:S(2)}) async-start(bf16[8,256,128]{2,1,0:T(8,128)(2,1)} %broadcast_in_dim.4), calls=%async_computation | async-start | bytes 1048576 | tf_op jit(solution)/shard_map/all_to_all | solution.py:300
  9.2 0.8 copy-start.6
  10.1 5.5 %collective-permute-start.2 = (bf16[512,128]{1,0:T(8,128)(2,1)S(1)}, bf16[512,128]{1,0:T(8,128)(2,1)S(1)}, u32[]{:S(2)}, u32[]{:S(2)}) collective-permute-start(bf16[512,128]{1,0:T(8,128)(2,1)S(1)} %constant_dynamic-update-slice_fusion), channel_id=1, source_target_pairs={{0,768},{1,769},{2,770},{3,771},{4,772},{5,773},{6,774},{7,775},{8... | collective-permute-start | bytes 393224 | tf_op jit(solution)/shard_map/ppermute | solution.py:299
  10.8 15.3 %collective-permute-start.1 = (bf16[512,128]{1,0:T(8,128)(2,1)S(1)}, bf16[512,128]{1,0:T(8,128)(2,1)S(1)}, u32[]{:S(2)}, u32[]{:S(2)}) collective-permute-start(bf16[512,128]{1,0:T(8,128)(2,1)S(1)} %constant_dynamic-update-slice_fusion), channel_id=1, source_target_pairs={{0,512},{256,768},{1,513},{257,769},{2,514},{258,770},{3,515},{259... | collective-permute-start | bytes 393224 | tf_op jit(solution)/shard_map/ppermute | solution.py:299
  12.1 17.2 %collective-permute-start = (bf16[512,128]{1,0:T(8,128)(2,1)S(1)}, bf16[512,128]{1,0:T(8,128)(2,1)S(1)}, u32[]{:S(2)}, u32[]{:S(2)}) collective-permute-start(bf16[512,128]{1,0:T(8,128)(2,1)S(1)} %constant_dynamic-update-slice_fusion), channel_id=1, source_target_pairs={{0,256},{256,512},{512,768},{1,257},{257,513},{513,769},{2,258},{2... | collective-permute-start | bytes 393224 | tf_op jit(solution)/shard_map/ppermute | solution.py:299
  29.4 4.0 %collective-permute-start.3 = (bf16[4,512,128]{2,1,0:T(8,128)(2,1)S(1)}, bf16[4,512,128]{2,1,0:T(8,128)(2,1)S(1)}, u32[]{:S(2)}, u32[]{:S(2)}) collective-permute-start(bf16[4,512,128]{2,1,0:T(8,128)(2,1)S(1)} %pad_maximum_fusion.own_ref), channel_id=1, source_target_pairs={{0,16},{16,0},{1,17},{17,1},{2,18},{18,2},{3,19},{19,3},{4,20},{20... | collective-permute-start | bytes 1572872 | tf_op jit(solution)/shard_map/ppermute | solution.py:302
  31.3 0.7 copy-start.7
  32.1 0.7 copy-start.4
  64.3 27.6 %copy-start.2 = (bf16[256,128]{1,0:T(8,128)(2,1)S(1)}, bf16[256,128]{1,0:T(8,128)(2,1)}, u32[]{:S(2)}) copy-start(bf16[256,128]{1,0:T(8,128)(2,1)} %c_ref.3) | copy-start | bytes 196612
  65.0 26.9 %copy-start = (bf16[256,128]{1,0:T(8,128)(2,1)S(1)}, bf16[256,128]{1,0:T(8,128)(2,1)}, u32[]{:S(2)}) copy-start(bf16[256,128]{1,0:T(8,128)(2,1)} %q_ref.3) | copy-start | bytes 196612
  65.0 26.9 %copy-start.1 = (bf16[256,128]{1,0:T(8,128)(2,1)S(1)}, bf16[256,128]{1,0:T(8,128)(2,1)}, u32[]{:S(2)}) copy-start(bf16[256,128]{1,0:T(8,128)(2,1)} %k_ref.3) | copy-start | bytes 196612
  91.9 12.1 %copy-start.3 = (f32[3,7,128]{2,1,0:T(8,128)S(1)}, f32[3,7,128]{2,1,0:T(8,128)}, u32[]{:S(2)}) copy-start(f32[3,7,128]{2,1,0:T(8,128)} %w_ref.1) | copy-start | bytes 32260
  92.2 11.9 %collective-permute-start.5 = (bf16[320,128]{1,0:T(8,128)(2,1)S(1)}, bf16[320,128]{1,0:T(8,128)(2,1)S(1)}, u32[]{:S(2)}, u32[]{:S(2)}) collective-permute-start(bf16[320,128]{1,0:T(8,128)(2,1)S(1)} %get-tuple-element.31), channel_id=1, source_target_pairs={{16,0},{32,16},{48,32},{64,48},{80,64},{96,80},{112,96},{128,112},... | collective-permute-start | bytes 245768 | tf_op jit(solution)/shard_map/ppermute | solution.py:291
  94.1 9.9 %collective-permute-start.4 = (bf16[304,128]{1,0:T(8,128)(2,1)S(1)}, bf16[304,128]{1,0:T(8,128)(2,1)S(1)}, u32[]{:S(2)}, u32[]{:S(2)}) collective-permute-start(bf16[304,128]{1,0:T(8,128)(2,1)S(1)} %get-tuple-element.30), channel_id=1, source_target_pairs={{0,16},{16,32},{32,48},{48,64},{64,80},{80,96},{96,112},{112,128},... | collective-permute-start | bytes 233480 | tf_op jit(solution)/shard_map/ppermute | solution.py:291

commit v2 on v1

--- a/solution.py
+++ b/solution.py
@@ -60,13 +60,6 @@
         return c
 
     lax.fori_loop(0, plane + 1, fill, 0)
-
-    def split(b, c):
-        acc_ref[b] = jnp.zeros((256, 256), F32)
-        m_ref[b] = jnp.full((256, 128), NEGATIVE, F32)
-        return c
-
-    lax.fori_loop(0, 8, split, 0)
 
     i = lax.broadcasted_iota(jnp.int32, (256, 256), 0)
     j = lax.broadcasted_iota(jnp.int32, (256, 256), 1)
@@ -87,37 +80,36 @@
         s_ref[n] = s
         t_ref[n] = jnp.broadcast_to(jnp.max(s, axis=1, keepdims=True), (256, 128))
 
-    def update(n, b, p):
-        old = m_ref[b]
-        new = jnp.maximum(old, rounded(t_ref[n]))
+    def update(n, b, p, first):
+        if first:
+            new = jnp.maximum(rounded(t_ref[n]), NEGATIVE)
+        else:
+            old = m_ref[b]
+            new = jnp.maximum(old, rounded(t_ref[n]))
+            scale = jnp.exp2(old - new)
         m_ref[b] = new
-        scale = jnp.exp2(old - new)
         e = jnp.concatenate([jnp.exp2(s_ref[n, :, 128 * k : 128 * k + 128] - new) for k in range(4)], axis=1)
         add = dot(e.astype(BF16), v_ref[p], ((1,), (0,)))
-        acc_ref[b, :, 0:128] = acc_ref[b, :, 0:128] * scale + add[:, 0:128]
-        acc_ref[b, :, 128:256] = acc_ref[b, :, 128:256] * scale + add[:, 128:256]
-
-    def some(first, p, masked):
+        if first:
+            acc_ref[b] = add
+        else:
+            acc_ref[b, :, 0:128] = acc_ref[b, :, 0:128] * scale + add[:, 0:128]
+            acc_ref[b, :, 128:256] = acc_ref[b, :, 128:256] * scale + add[:, 128:256]
+
+    def every(p, first):
         for n in range(8):
-            scores(n, first + n, p, masked)
+            scores(n, n, p, first)
             if n:
-                update(n - 1, first + n - 1, p)
-        update(8 - 1, first + 8 - 1, p)
-
-    def same(g, c):
-        @pl.when(8 * (g + 1) > column)
-        def _():
-            some(8 * g, 0, True)
-
+                update(n - 1, n - 1, p, first)
+        update(7, 7, p, first)
+
+    every(0, True)
+
+    def past(p, c):
+        every(p, False)
         return c
 
-    lax.fori_loop(0, 8 // 8, same, 0)
-
-    def past(g, c):
-        some(8 * lax.rem(g, 8 // 8), 1 + lax.div(g, 8 // 8), False)
-        return c
-
-    lax.fori_loop(0, plane * (8 // 8), past, 0)
+    lax.fori_loop(1, plane + 1, past, 0)
 
     def emit(b, c):
         o_ref[b, 0:256, :] = acc_ref[b, :, 0:128].astype(BF16)

time: 106 us -> 106 us (level)
  no operation moved by 1% of the time
where the time goes in v2:
time: 106 us; the launch traced here: 105 us
  blocking collectives  52.1 us (49%)
  waiting for transfers between devices  21.2 us (20%)
  starting transfers between devices  18.6 us (18%)
  Pallas kernels  8.61 us (8%)
  local copies, waits for them, and re-layouts  4.03 us (4%)
    all_to_all x1, blocking collectives, per_device(): squares = lax.all_to_all(sums, HEAD, 0, 0, tiled=True)  26.8 us
    all_to_all x1, blocking collectives, per_device(): parts = lax.all_to_all(partial, 'x', 0, 0, tiled=True)  25.2 us
    ppermute x3, waiting for transfers between devices, per_device(): came.append(lax.ppermute(both, 'y_hi', [(i, i + d) for i in range(4 - d)]))  13.6 us
    pallas_call x5, Pallas kernels, call(): pl.pallas_call(body, out_shape=outs, in_specs=specs or [VM] * len(args),...  8.61 us
    ppermute x2, waiting for transfers between devices, neighbour(): lax.ppermute(block, CTX, [(i, i + distance) for i in range(n) if 0 <= i +...  7.52 us
    all_to_all x1, starting transfers between devices, per_device(): lax.all_to_all(jnp.broadcast_to(q_att[None], (8, BLOCK, HD)), 'x', 0, 0,...  6.89 us
    ppermute x3, starting transfers between devices, per_device(): came.append(lax.ppermute(both, 'y_hi', [(i, i + d) for i in range(4 - d)]))  5.51 us
    ppermute x2, starting transfers between devices, neighbour(): lax.ppermute(block, CTX, [(i, i + distance) for i in range(n) if 0 <= i +...  4.33 us
  transfers between devices with their start and end apart: 7, of which 3 were waited for; matrix products, arithmetic and copies ran while one was open for 0% of the time, Pallas kernels for 0%

profile of v2, /device:TPU:64, one launch (start us, length us, event | category | flops | bytes accessed | tf_op | source)
XLA Modules:
  0.0 105.5 jit_solution(17917770933744501499)
XLA Ops:
  0.6 1.7 %broadcast_in_dim.4 = bf16[8,256,128]{2,1,0:T(8,128)(2,1)} broadcast(bf16[256,128]{1,0:T(8,128)(2,1)} %param.9), dimensions={1,2} | broadcast | bytes 589824 | tf_op jit(solution)/shard_map/broadcast_in_dim | solution.py:292
  2.3 6.9 %all-to-all-start = ((bf16[8,256,128]{2,1,0:T(8,128)(2,1)}), bf16[8,256,128]{2,1,0:T(8,128)(2,1)S(1)}, u32[]{:S(2)}, u32[]{:S(2)}) async-start(bf16[8,256,128]{2,1,0:T(8,128)(2,1)} %broadcast_in_dim.4), calls=%async_computation | async-start | bytes 1048576 | tf_op jit(solution)/shard_map/all_to_all | solution.py:292
  9.2 0.0 copy-start.6
  9.3 0.8 copy-done.6
  10.1 0.7 collective-permute-start.2
  10.8 1.3 %collective-permute-start.1 = (bf16[512,128]{1,0:T(8,128)(2,1)S(1)}, bf16[512,128]{1,0:T(8,128)(2,1)S(1)}, u32[]{:S(2)}, u32[]{:S(2)}) collective-permute-start(bf16[512,128]{1,0:T(8,128)(2,1)S(1)} %constant_dynamic-update-slice_fusion), channel_id=1, source_target_pairs={{0,512},{256,768},{1,513},{257,769},{2,514},{258,770},{3,515},{259... | collective-permute-start | bytes 393224 | tf_op jit(solution)/shard_map/ppermute | solution.py:291
  12.1 3.5 %collective-permute-start = (bf16[512,128]{1,0:T(8,128)(2,1)S(1)}, bf16[512,128]{1,0:T(8,128)(2,1)S(1)}, u32[]{:S(2)}, u32[]{:S(2)}) collective-permute-start(bf16[512,128]{1,0:T(8,128)(2,1)S(1)} %constant_dynamic-update-slice_fusion), channel_id=1, source_target_pairs={{0,256},{256,512},{512,768},{1,257},{257,513},{513,769},{2,258},{2... | collective-permute-start | bytes 393224 | tf_op jit(solution)/shard_map/ppermute | solution.py:291
  15.6 0.0 collective-permute-done.2
  15.6 10.4 %collective-permute-done.1 = bf16[512,128]{1,0:T(8,128)(2,1)S(1)} collective-permute-done((bf16[512,128]{1,0:T(8,128)(2,1)S(1)}, bf16[512,128]{1,0:T(8,128)(2,1)S(1)}, u32[]{:S(2)}, u32[]{:S(2)}) %collective-permute-start.1) | collective-permute-done | bytes 131104 | tf_op jit(solution)/shard_map/ppermute | solution.py:291
  26.1 3.2 %collective-permute-done = bf16[512,128]{1,0:T(8,128)(2,1)S(1)} collective-permute-done((bf16[512,128]{1,0:T(8,128)(2,1)S(1)}, bf16[512,128]{1,0:T(8,128)(2,1)S(1)}, u32[]{:S(2)}, u32[]{:S(2)}) %collective-permute-start) | collective-permute-done | bytes 131104 | tf_op jit(solution)/shard_map/ppermute | solution.py:291
  29.3 0.1 pad_maximum_fusion.own_ref
  29.4 1.9 %collective-permute-start.3 = (bf16[4,512,128]{2,1,0:T(8,128)(2,1)S(1)}, bf16[4,512,128]{2,1,0:T(8,128)(2,1)S(1)}, u32[]{:S(2)}, u32[]{:S(2)}) collective-permute-start(bf16[4,512,128]{2,1,0:T(8,128)(2,1)S(1)} %pad_maximum_fusion.own_ref), channel_id=1, source_target_pairs={{0,16},{16,0},{1,17},{17,1},{2,18},{18,2},{3,19},{19,3},{4,20},{20... | collective-permute-start | bytes 1572872 | tf_op jit(solution)/shard_map/ppermute | solution.py:294
  31.3 0.0 copy-start.7
  31.3 0.7 copy-done.7
  32.0 0.1 copy.13.f_ref
  32.1 0.7 copy-done.4
  32.7 0.5 shard_map.120
  33.3 0.1 pad_add_fusion.info
  33.3 0.0 collective-permute-done.3.oth_ref
  33.3 0.0 all-to-all-done.q_ref
  33.3 5.4 %shard_map.121 = bf16[8,264,128]{2,1,0:T(8,128)(2,1)S(1)} custom-call(s32[4]{0:T(128)S(1)} %pad_add_fusion.info, bf16[8,256,128]{2,1,0:T(8,128)(2,1)S(1)} %all-to-all-done.q_ref, bf16[4,512,128]{2,1,0:T(8,128)(2,1)S(1)} %pad_maximum_fusion.own_ref, bf16[4,512,128]{2,1,0:T(8,128)(2,1)S(1)} %collective-permute-done.3.oth_ref), custom_call_target="tpu_custom_call" | custom-call | flops 4000000000 | bytes 1048576 | tf_op jit(solution)/shard_map/pallas_call | solution.py:266
  38.8 25.2 %all_to_all.15.msg_ref = bf16[8,264,128]{2,1,0:T(8,128)(2,1)S(1)} all-to-all(bf16[8,264,128]{2,1,0:T(8,128)(2,1)S(1)} %shard_map.121), channel_id=1, replica_groups=mesh['y_hi'=4,'x'=8,'core'=2,'y_lo'=2,'z'=8] {'x'}, dimensions={0} | all-to-all | bytes 1081344 | tf_op jit(solution)/shard_map/all_to_all | solution.py:318
  64.0 0.7 shard_map.122
  64.7 0.0 copy-start.1
  64.7 26.8 %all_to_all.16.s_ref = f32[16,8,128]{2,1,0:T(8,128)S(1)} all-to-all(f32[16,8,128]{2,1,0:T(8,128)S(1)} %get-tuple-element.27), channel_id=1, replica_groups=mesh['y_hi'=4,'x'=8,'core'=2,'y_lo'=2,'z'=8] {'y_lo','z'}, dimensions={0} | all-to-all | bytes 131072 | tf_op jit(solution)/shard_map/all_to_all | solution.py:320
  91.6 0.0 copy-start.3
  91.6 0.2 shard_map.123
  91.9 1.9 %collective-permute-start.5 = (bf16[320,128]{1,0:T(8,128)(2,1)S(1)}, bf16[320,128]{1,0:T(8,128)(2,1)S(1)}, u32[]{:S(2)}, u32[]{:S(2)}) collective-permute-start(bf16[320,128]{1,0:T(8,128)(2,1)S(1)} %get-tuple-element.31), channel_id=1, source_target_pairs={{16,0},{32,16},{48,32},{64,48},{80,64},{96,80},{112,96},{128,112},... | collective-permute-start | bytes 245768 | tf_op jit(solution)/shard_map/ppermute | solution.py:283
  93.8 2.4 %collective-permute-start.4 = (bf16[304,128]{1,0:T(8,128)(2,1)S(1)}, bf16[304,128]{1,0:T(8,128)(2,1)S(1)}, u32[]{:S(2)}, u32[]{:S(2)}) collective-permute-start(bf16[304,128]{1,0:T(8,128)(2,1)S(1)} %get-tuple-element.30), channel_id=1, source_target_pairs={{0,16},{16,32},{32,48},{48,64},{64,80},{80,96},{96,112},{112,128},... | collective-permute-start | bytes 233480 | tf_op jit(solution)/shard_map/ppermute | solution.py:283
  96.2 7.5 %collective-permute-done.4.before_ref = bf16[304,128]{1,0:T(8,128)(2,1)S(1)} collective-permute-done((bf16[304,128]{1,0:T(8,128)(2,1)S(1)}, bf16[304,128]{1,0:T(8,128)(2,1)S(1)}, u32[]{:S(2)}, u32[]{:S(2)}) %collective-permute-start.4) | collective-permute-done | bytes 77856 | tf_op jit(solution)/shard_map/ppermute | solution.py:283
  103.7 0.0 collective-permute-done.5.after_ref
  103.7 1.7 %shard_map.124 = (bf16[256,128]{1,0:T(8,128)(2,1)}, bf16[256,128]{1,0:T(8,128)(2,1)}, bf16[256,128]{1,0:T(8,128)(2,1)}, bf16[256,128]{1,0:T(8,128)(2,1)}) custom-call(bf16[256,128]{1,0:T(8,128)(2,1)S(1)} %get-tuple-element.29.v_ref, bf16[256,128]{1,0:T(8,128)(2,1)S(1)} %copy-done, bf16[256,128]{1,0:T(8,128)(2,1)S(1)} %copy-done.1, ...), custom_call_target="tpu_custom_call" | custom-call | bytes 1048576 | tf_op jit(solution)/shard_map/pallas_call | solution.py:266
  (11 shorter events, 0.0 us)
Async XLA Ops:
  2.3 6.9 %copy-start.5 = (bf16[256,128]{1,0:T(8,128)(2,1)S(1)}, bf16[256,128]{1,0:T(8,128)(2,1)}, u32[]{:S(2)}) copy-start(bf16[256,128]{1,0:T(8,128)(2,1)} %param.10) | copy-start | bytes 196612
  2.3 31.0 %all-to-all-start = ((bf16[8,256,128]{2,1,0:T(8,128)(2,1)}), bf16[8,256,128]{2,1,0:T(8,128)(2,1)S(1)}, u32[]{:S(2)}, u32[]{:S(2)}) async-start(bf16[8,256,128]{2,1,0:T(8,128)(2,1)} %broadcast_in_dim.4), calls=%async_computation | async-start | bytes 1048576 | tf_op jit(solution)/shard_map/all_to_all | solution.py:292
  9.2 0.8 copy-start.6
  10.1 5.5 %collective-permute-start.2 = (bf16[512,128]{1,0:T(8,128)(2,1)S(1)}, bf16[512,128]{1,0:T(8,128)(2,1)S(1)}, u32[]{:S(2)}, u32[]{:S(2)}) collective-permute-start(bf16[512,128]{1,0:T(8,128)(2,1)S(1)} %constant_dynamic-update-slice_fusion), channel_id=1, source_target_pairs={{0,768},{1,769},{2,770},{3,771},{4,772},{5,773},{6,774},{7,775},{8... | collective-permute-start | bytes 393224 | tf_op jit(solution)/shard_map/ppermute | solution.py:291
  10.8 15.3 %collective-permute-start.1 = (bf16[512,128]{1,0:T(8,128)(2,1)S(1)}, bf16[512,128]{1,0:T(8,128)(2,1)S(1)}, u32[]{:S(2)}, u32[]{:S(2)}) collective-permute-start(bf16[512,128]{1,0:T(8,128)(2,1)S(1)} %constant_dynamic-update-slice_fusion), channel_id=1, source_target_pairs={{0,512},{256,768},{1,513},{257,769},{2,514},{258,770},{3,515},{259... | collective-permute-start | bytes 393224 | tf_op jit(solution)/shard_map/ppermute | solution.py:291
  12.1 17.2 %collective-permute-start = (bf16[512,128]{1,0:T(8,128)(2,1)S(1)}, bf16[512,128]{1,0:T(8,128)(2,1)S(1)}, u32[]{:S(2)}, u32[]{:S(2)}) collective-permute-start(bf16[512,128]{1,0:T(8,128)(2,1)S(1)} %constant_dynamic-update-slice_fusion), channel_id=1, source_target_pairs={{0,256},{256,512},{512,768},{1,257},{257,513},{513,769},{2,258},{2... | collective-permute-start | bytes 393224 | tf_op jit(solution)/shard_map/ppermute | solution.py:291
  29.4 4.0 %collective-permute-start.3 = (bf16[4,512,128]{2,1,0:T(8,128)(2,1)S(1)}, bf16[4,512,128]{2,1,0:T(8,128)(2,1)S(1)}, u32[]{:S(2)}, u32[]{:S(2)}) collective-permute-start(bf16[4,512,128]{2,1,0:T(8,128)(2,1)S(1)} %pad_maximum_fusion.own_ref), channel_id=1, source_target_pairs={{0,16},{16,0},{1,17},{17,1},{2,18},{18,2},{3,19},{19,3},{4,20},{20... | collective-permute-start | bytes 1572872 | tf_op jit(solution)/shard_map/ppermute | solution.py:294
  31.3 0.7 copy-start.7
  32.1 0.7 copy-start.4
  64.0 27.6 %copy-start.2 = (bf16[256,128]{1,0:T(8,128)(2,1)S(1)}, bf16[256,128]{1,0:T(8,128)(2,1)}, u32[]{:S(2)}) copy-start(bf16[256,128]{1,0:T(8,128)(2,1)} %c_ref.3) | copy-start | bytes 196612
  64.7 26.9 %copy-start = (bf16[256,128]{1,0:T(8,128)(2,1)S(1)}, bf16[256,128]{1,0:T(8,128)(2,1)}, u32[]{:S(2)}) copy-start(bf16[256,128]{1,0:T(8,128)(2,1)} %q_ref.3) | copy-start | bytes 196612
  64.7 26.9 %copy-start.1 = (bf16[256,128]{1,0:T(8,128)(2,1)S(1)}, bf16[256,128]{1,0:T(8,128)(2,1)}, u32[]{:S(2)}) copy-start(bf16[256,128]{1,0:T(8,128)(2,1)} %k_ref.3) | copy-start | bytes 196612
  91.6 12.1 %copy-start.3 = (f32[3,7,128]{2,1,0:T(8,128)S(1)}, f32[3,7,128]{2,1,0:T(8,128)}, u32[]{:S(2)}) copy-start(f32[3,7,128]{2,1,0:T(8,128)} %w_ref.1) | copy-start | bytes 32260
  91.9 11.9 %collective-permute-start.5 = (bf16[320,128]{1,0:T(8,128)(2,1)S(1)}, bf16[320,128]{1,0:T(8,128)(2,1)S(1)}, u32[]{:S(2)}, u32[]{:S(2)}) collective-permute-start(bf16[320,128]{1,0:T(8,128)(2,1)S(1)} %get-tuple-element.31), channel_id=1, source_target_pairs={{16,0},{32,16},{48,32},{64,48},{80,64},{96,80},{112,96},{128,112},... | collective-permute-start | bytes 245768 | tf_op jit(solution)/shard_map/ppermute | solution.py:283
  93.8 9.9 %collective-permute-start.4 = (bf16[304,128]{1,0:T(8,128)(2,1)S(1)}, bf16[304,128]{1,0:T(8,128)(2,1)S(1)}, u32[]{:S(2)}, u32[]{:S(2)}) collective-permute-start(bf16[304,128]{1,0:T(8,128)(2,1)S(1)} %get-tuple-element.30), channel_id=1, source_target_pairs={{0,16},{16,32},{32,48},{48,64},{64,80},{80,96},{96,112},{112,128},... | collective-permute-start | bytes 233480 | tf_op jit(solution)/shard_map/ppermute | solution.py:283
